TPU v7x, 32 devices: a whole 2x2x4 slice. The times are simulated.
32 devices in a mesh: row: 8 (over y, x, core), col: 4 (over z).
Axes of the slice: x: 2, y: 2, z: 4, core: 2. Of those that a mesh axis runs over, the one named last changes fastest.
Arguments:
- amplitudes: bfloat16 [24576, 24576], P('col', 'row'), may hold values from -0.0390625 to 0.0390625
- cholesky: bfloat16 [24576, 1280], P(('row', 'col')), may hold values from -5 to 5
- occ_map: int32 [24576], replicated, may hold values from 0 to 47
- vir_map: int32 [24576], replicated, may hold values from 0 to 511
Outputs:
- new_amplitudes: bfloat16 [24576, 24576], P('col', 'row')
All inputs are finite; a program needn't handle non-finite values.
Results may differ from a plain program's by a relative error of at most 0.0056.
Values may be sent and summed in bfloat16 or wider, within the bound.
No kernel may reach another device: no remote copies, remote signals or barrier semaphores. Data moves between devices by JAX's collectives and lax.ppermute only.
A program may use at most 192 MiB of HBM per device.

v0:
```python
import jax
import jax.numpy as jnp
from jax import lax
from jax.sharding import PartitionSpec as P

NOCC = 48
NVIR = 512


def broadcast(x, axis, root):
    mine = lax.axis_index(axis) == root
    return lax.psum(jnp.where(mine, x, jnp.zeros_like(x)), axis)


def pair_gap(occ_map, vir_map):
    occ = occ_map.astype(jnp.float32)
    vir = vir_map.astype(jnp.float32)
    return 0.5 + 2.5 * jnp.sqrt(vir / NVIR) + (0.5 + 2.5 * occ / NOCC)


def body(amplitudes, cholesky, occ_map, vir_map):
    tile_rows, tile_cols = amplitudes.shape
    row_index = lax.axis_index("row")
    col_index = lax.axis_index("col")
    q_start = row_index * tile_cols
    p_start = col_index * tile_rows
    offset = q_start - p_start
    on_diag = jnp.logical_and(offset >= 0, offset < tile_rows).astype(jnp.float32)
    safe_offset = jnp.clip(offset, 0, tile_rows - tile_cols)
    piece = lax.all_gather(cholesky, "col", axis=0, tiled=True)
    count = piece.shape[0]
    total = jnp.dot(amplitudes, piece, preferred_element_type=jnp.float32)
    current = lax.dynamic_slice_in_dim(total, safe_offset, count, 0)
    partial_value = lax.dynamic_update_slice_in_dim(
        total, current + on_diag * piece.astype(jnp.float32), safe_offset, 0
    )
    y_share = lax.psum_scatter(partial_value, "row", scatter_dimension=0, tiled=True).astype(
        jnp.bfloat16
    )
    y_block = lax.all_gather(y_share, "row", axis=0, tiled=True)
    q_root = q_start // tile_rows
    q_inside = q_start % tile_rows
    own_part = lax.dynamic_slice_in_dim(y_block, q_inside, tile_cols, 0)
    y_cols = broadcast(own_part, "col", q_root)
    cycle = lax.dot_general(
        y_block, y_cols, (((1,), (1,)), ((), ())), preferred_element_type=jnp.float32
    )
    gap_rows = pair_gap(
        lax.dynamic_slice_in_dim(occ_map, p_start, tile_rows, 0),
        lax.dynamic_slice_in_dim(vir_map, p_start, tile_rows, 0),
    )
    gap_cols = pair_gap(
        lax.dynamic_slice_in_dim(occ_map, q_start, tile_cols, 0),
        lax.dynamic_slice_in_dim(vir_map, q_start, tile_cols, 0),
    )
    return (-cycle / (gap_rows[:, None] + gap_cols[None, :])).astype(jnp.bfloat16)


def solution(mesh):
    return jax.shard_map(
        body,
        mesh=mesh,
        in_specs=(P("col", "row"), P(("row", "col"), None), P(), P()),
        out_specs=P("col", "row"),
        check_vma=False,
    )
```

profile of v0, /device:TPU:0, one launch (start us, length us, event | category | flops | bytes accessed | tf_op | source)
XLA Modules:
  0.0 884.4 jit_solution(14098019015922236109)
XLA Ops:
  6.5 0.0 all-gather.3.cloned.1.call-start
  6.5 0.7 all-gather.3.cloned.1.call-update
  7.3 0.0 reduce-scatter.2.cloned.1.call-start
  7.3 145.4 %all-gather.3.cloned.1.call-done = bf16[3072,1280]{1,0:T(8,128)(2,1)} async-done(((bf16[768,1280]{1,0:T(8,128)(2,1)}), bf16[3072,1280]{1,0:T(8,128)(2,1)}) %all-gather.3.cloned.1.call-update) | async-done | bytes 7864336 | tf_op jit(solution)/shard_map/all_gather | solution.py:30
  152.7 0.0 copy-start
  152.7 58.6 %fusion = f32[6144,1280]{1,0:T(8,128)} fusion(bf16[6144,3072]{1,0:T(8,128)(2,1)} %param.4, bf16[3072,1280]{1,0:T(8,128)(2,1)} %all-gather.3.cloned.1.call-done), kind=kOutput, calls=%fused_computation.5 | convolution fusion | flops 48318382080 | bytes 77070336 | tf_op jit(solution)/shard_map/dot_general | solution.py:32
  211.3 0.0 copy-done
  211.3 11.6 %multiply_add_fusion = f32[3072,1280]{1,0:T(8,128)} fusion(bf16[3072,1280]{1,0:T(8,128)(2,1)S(1)} %copy-done, f32[6144,1280]{1,0:T(8,128)} %fusion, s32[]{:T(128)S(6)} %min.4, f32[]{:T(128)S(6)} %convert_element_type.24), kind=kLoop, calls=%fused_computation.1 | loop fusion | flops 11796480 | bytes 39321608 | tf_op jit(solution)/shard_map/add | solution.py:35
  222.9 36.3 %dynamic_update_slice.3 = f32[6144,1280]{1,0:T(8,128)} dynamic-update-slice(f32[6144,1280]{1,0:T(8,128)} %fusion, f32[3072,1280]{1,0:T(8,128)} %multiply_add_fusion, s32[]{:T(128)S(6)} %min.4, s32[]{:T(128)} %constant.40.clone.1) | dynamic-update-slice | bytes 31457284 | tf_op jit(solution)/shard_map/dynamic_update_slice | solution.py:34
  259.2 0.0 reduce-scatter.2.cloned.1.call-update
  259.2 0.0 all-gather.5.cloned.1.call-start
  259.3 190.0 %reduce-scatter.2.cloned.1.call-done = f32[768,1280]{1,0:T(8,128)} async-done(((f32[6144,1280]{1,0:T(8,128)}), f32[768,1280]{1,0:T(8,128)}) %reduce-scatter.2.cloned.1.call-update) | async-done | bytes 3932176 | tf_op jit(solution)/shard_map/reduce_scatter | solution.py:37
  449.3 3.6 convert_element_type.26
  452.8 0.0 all-gather.5.cloned.1.call-update
  452.9 0.2 all-reduce.2.cloned.1.call-start
  453.1 85.2 %all-gather.5.cloned.1.call-done = bf16[6144,1280]{1,0:T(8,128)(2,1)} async-done(((bf16[768,1280]{1,0:T(8,128)(2,1)}), bf16[6144,1280]{1,0:T(8,128)(2,1)}) %all-gather.5.cloned.1.call-update) | async-done | bytes 15728656 | tf_op jit(solution)/shard_map/all_gather | solution.py:40
  538.3 8.8 dynamic-slice_select_fusion
  547.2 0.0 all-reduce.2.cloned.1.call-update
  547.2 0.7 add_add_fusion.1
  547.9 0.8 add_add_fusion
  548.7 272.4 %all-reduce.2.cloned.1.call-done = bf16[3072,1280]{1,0:T(8,128)(2,1)} async-done(((bf16[3072,1280]{1,0:T(8,128)(2,1)}), bf16[3072,1280]{1,0:T(8,128)(2,1)}) %all-reduce.2.cloned.1.call-update) | async-done | bytes 7864336 | tf_op jit(solution)/shard_map/psum | solution.py:12
  821.1 56.7 %divide_convert_fusion = bf16[6144,3072]{1,0:T(8,128)(2,1)} fusion(bf16[6144,1280]{1,0:T(8,128)(2,1)} %all-gather.5.cloned.1.call-done, bf16[3072,1280]{1,0:T(8,128)(2,1)} %all-reduce.2.cloned.1.call-done, f32[3072]{0:T(1024)S(1)} %add_add_fusion.1, f32[6144]{0:T(1024)S(1)} %add_add_fusion), kind=kOutput, calls=%fused_computation | convolution fusion | flops 48393879552 | bytes 61378560 | tf_op jit(solution)/shard_map/dot_general | solution.py:45
Async XLA Ops:
  6.5 146.2 %all-gather.3.cloned.1.call-start = ((), (), s32[]{:S(2)}) async-start(), calls=%async_computation.1 | async-start | bytes 9830400 | tf_op jit(solution)/shard_map/all_gather | solution.py:30
  7.3 442.0 %reduce-scatter.2.cloned.1.call-start = ((), (), s32[]{:S(2)}) async-start(), calls=%async_computation.2 | async-start | bytes 35389440 | tf_op jit(solution)/shard_map/reduce_scatter | solution.py:37
  152.7 58.6 %copy-start = (bf16[3072,1280]{1,0:T(8,128)(2,1)S(1)}, bf16[3072,1280]{1,0:T(8,128)(2,1)}, u32[]{:S(2)}) copy-start(bf16[3072,1280]{1,0:T(8,128)(2,1)} %all-gather.3.cloned.1.call-done) | copy-start | bytes 23592964
  259.2 279.1 %all-gather.5.cloned.1.call-start = ((), (), s32[]{:S(2)}) async-start(), calls=%async_computation.3 | async-start | bytes 17694720 | tf_op jit(solution)/shard_map/all_gather | solution.py:40
  452.9 368.2 %all-reduce.2.cloned.1.call-start = ((), (), s32[]{:S(2)}) async-start(), calls=%async_computation.4 | async-start | bytes 15728640 | tf_op jit(solution)/shard_map/psum | solution.py:12
Sparse Core Ops, SparseCore 0:
  8.9 143.7 all-gather.2
  259.4 189.8 reduce-scatter.1
  453.0 85.3 all-gather.4
  547.3 273.7 all-reduce.1
where the time goes:
time: 886 us; the launch traced here: 884 us
  waiting for transfers between devices  694 us (78%)
  matrix products  115 us (13%)
  local copies, waits for them, and re-layouts  36.3 us (4%)
  other arithmetic  25.5 us (3%)
  between operations  13.2 us (1%)
    psum x1, waiting for transfers between devices, broadcast(): return lax.psum(jnp.where(mine, x, jnp.zeros_like(x)), axis)  272 us
    reduce_scatter x1, waiting for transfers between devices, body(): lax.psum_scatter(partial_value, 'row', scatter_dimension=0, tiled=True)  190 us
    all_gather x1, waiting for transfers between devices, body(): piece = lax.all_gather(cholesky, 'col', axis=0, tiled=True)  145 us
    all_gather x1, waiting for transfers between devices, body(): y_block = lax.all_gather(y_share, 'row', axis=0, tiled=True)  85.2 us
    dot_general x1, matrix products, body(): total = jnp.dot(amplitudes, piece, preferred_element_type=jnp.float32)  58.6 us
    dot_general x1, matrix products, body(): lax.dot_general(y_block, y_cols, (((1,), (1,)), ((), ())), preferred_elem...  56.7 us
    dynamic_update_slice x1, local copies, waits for them, and re-layouts, body(): lax.dynamic_update_slice_in_dim(total, current + on_diag * piece.astype(j...  36.3 us
  transfers between devices with their start and end apart: 4, of which 4 were waited for; matrix products, arithmetic and copies ran while one was open for 0% of the time, Pallas kernels for 0%

commit v1 on v0

--- a/solution.py
+++ b/solution.py
@@ -5,6 +5,28 @@
 
 NOCC = 48
 NVIR = 512
+
+
+def in_order(parts, dim):
+    parts = jnp.moveaxis(parts, 0, dim)
+    dims = parts.shape
+    return parts.reshape(*dims[:dim], dims[dim] * dims[dim + 1], *dims[dim + 2 :])
+
+
+def collect(x, axis, dim):
+    length = lax.axis_size(axis)
+    pairs = [(i, (i + 1) % length) for i in range(length)]
+    back = [(b, a) for a, b in pairs]
+    lower, upper = ([], [])
+    for turn in range(length - 1):
+        if turn % 2 == 0:
+            lower.append(lax.ppermute(lower[-1] if lower else x, axis, pairs))
+        else:
+            upper.append(lax.ppermute(upper[-1] if upper else x, axis, back))
+    parts = jnp.stack([*lower[::-1], x, *upper])
+    shift = lax.axis_index(axis) - len(lower)
+    parts = parts[(jnp.arange(length) - shift) % length]
+    return in_order(parts, dim)
 
 
 def broadcast(x, axis, root):
@@ -27,7 +49,7 @@
     offset = q_start - p_start
     on_diag = jnp.logical_and(offset >= 0, offset < tile_rows).astype(jnp.float32)
     safe_offset = jnp.clip(offset, 0, tile_rows - tile_cols)
-    piece = lax.all_gather(cholesky, "col", axis=0, tiled=True)
+    piece = collect(cholesky, "col", 0)
     count = piece.shape[0]
     total = jnp.dot(amplitudes, piece, preferred_element_type=jnp.float32)
     current = lax.dynamic_slice_in_dim(total, safe_offset, count, 0)

time: 886 us -> 934 us (1.054)
  local copies, waits for them, and re-layouts: 36.3 us -> 86.5 us
  waiting for transfers between devices: 694 us -> 670 us
  other arithmetic: 25.5 us -> 35.7 us
    all_gather x1 -> x0, waiting for transfers between devices: 145 us -> none  [body(): piece = lax.all_gather(cholesky, 'col', axis=0, tiled=True)]
    ppermute x0 -> x3, waiting for transfers between devices: none -> 127 us  [the longest x2 86.4 us: collect(): lower.append(lax.ppermute(lower[-1] if lower else x, axis, pairs))]
    dynamic_update_slice x1, local copies, waits for them, and re-layouts: 36.3 us -> 68.2 us  [body(): lax.dynamic_update_slice_in_dim(total, current + on_diag * piece.astype(j...]
    reshape x0 -> x1, local copies, waits for them, and re-layouts: none -> 10.6 us  [in_order(): parts.reshape(*dims[:dim], dims[dim] * dims[dim + 1], *dims[dim + 2:])]
  transfers between devices with their start and end apart: 4 -> 6, of which waited for: 4 -> 6; matrix products, arithmetic and copies ran while one was open for 0% -> 0% of each run, Pallas kernels for 0% -> 0%
where the time goes in v1:
time: 934 us; the launch traced here: 932 us
  waiting for transfers between devices  670 us (72%)
  matrix products  121 us (13%)
  local copies, waits for them, and re-layouts  86.5 us (9%)
  other arithmetic  35.7 us (4%)
  between operations  13.2 us (1%)
    psum x1, waiting for transfers between devices, broadcast(): return lax.psum(jnp.where(mine, x, jnp.zeros_like(x)), axis)  272 us
    reduce_scatter x1, waiting for transfers between devices, body(): lax.psum_scatter(partial_value, 'row', scatter_dimension=0, tiled=True)  185 us
    ppermute x2, waiting for transfers between devices, collect(): lower.append(lax.ppermute(lower[-1] if lower else x, axis, pairs))  86.4 us
    all_gather x1, waiting for transfers between devices, body(): y_block = lax.all_gather(y_share, 'row', axis=0, tiled=True)  84.8 us
    dynamic_update_slice x1, local copies, waits for them, and re-layouts, body(): lax.dynamic_update_slice_in_dim(total, current + on_diag * piece.astype(j...  68.2 us
    dot_general x1, matrix products, body(): lax.dot_general(y_block, y_cols, (((1,), (1,)), ((), ())), preferred_elem...  63.1 us
    dot_general x1, matrix products, body(): total = jnp.dot(amplitudes, piece, preferred_element_type=jnp.float32)  57.9 us
    ppermute x1, waiting for transfers between devices, collect(): upper.append(lax.ppermute(upper[-1] if upper else x, axis, back))  41 us
  transfers between devices with their start and end apart: 6, of which 6 were waited for; matrix products, arithmetic and copies ran while one was open for 0% of the time, Pallas kernels for 0%

profile of v1, /device:TPU:0, one launch (start us, length us, event | category | flops | bytes accessed | tf_op | source)
XLA Modules:
  0.0 931.6 jit_solution(11507082503690203928)
XLA Ops:
  6.5 0.0 reduce-scatter.2.cloned.1.call-start
  6.5 3.1 collective-permute-start
  9.6 2.0 collective-permute-start.2
  11.6 43.9 %collective-permute-done = bf16[768,1280]{1,0:T(8,128)(2,1)S(1)} collective-permute-done((bf16[768,1280]{1,0:T(8,128)(2,1)}, bf16[768,1280]{1,0:T(8,128)(2,1)S(1)}, u32[]{:S(2)}, u32[]{:S(2)}) %collective-permute-start) | collective-permute-done | bytes 1966112 | tf_op jit(solution)/shard_map/ppermute | solution.py:23
  55.5 0.0 collective-permute-start.1
  55.6 41.0 %collective-permute-done.2 = bf16[768,1280]{1,0:T(8,128)(2,1)} collective-permute-done((bf16[768,1280]{1,0:T(8,128)(2,1)}, bf16[768,1280]{1,0:T(8,128)(2,1)}, u32[]{:S(2)}, u32[]{:S(2)}) %collective-permute-start.2) | collective-permute-done | bytes 1966112 | tf_op jit(solution)/shard_map/ppermute | solution.py:25
  96.6 42.5 %collective-permute-done.1 = bf16[768,1280]{1,0:T(8,128)(2,1)} collective-permute-done((bf16[768,1280]{1,0:T(8,128)(2,1)S(1)}, bf16[768,1280]{1,0:T(8,128)(2,1)}, u32[]{:S(2)}, u32[]{:S(2)}) %collective-permute-start.1) | collective-permute-done | bytes 1966112 | tf_op jit(solution)/shard_map/ppermute | solution.py:23
  139.1 6.4 pad_maximum_fusion
  145.4 7.7 gather_fusion
  153.1 10.6 %copy.6 = bf16[3072,1280]{0,1:T(8,128)(2,1)} copy(bf16[3072,1280]{1,0:T(8,128)(2,1)} %bitcast.15) | data formatting | bytes 15728640 | tf_op jit(solution)/shard_map/reshape | solution.py:13
  163.7 0.0 copy-start
  163.7 57.9 %fusion.2 = f32[1280,6144]{1,0:T(8,128)} fusion(bf16[3072,1280]{1,0:T(8,128)(2,1)} %bitcast.16, bf16[6144,3072]{1,0:T(8,128)(2,1)} %param.4), kind=kOutput, calls=%fused_computation.14 | convolution fusion | flops 48318382080 | bytes 77070336 | tf_op jit(solution)/shard_map/dot_general | solution.py:54
  221.6 0.0 copy-done
  221.6 12.6 %bitcast_add_fusion = f32[3072,1280]{0,1:T(8,128)} fusion(bf16[3072,1280]{0,1:T(8,128)(2,1)S(1)} %copy-done, f32[1280,6144]{1,0:T(8,128)} %fusion.2, s32[]{:T(128)S(6)} %min.4, f32[]{:T(128)S(6)} %convert_element_type.24), kind=kLoop, calls=%fused_computation.2 | loop fusion | flops 11796480 | bytes 39321608 | tf_op jit(solution)/shard_map/add | solution.py:57
  234.2 68.2 %dynamic_update_slice.3 = f32[6144,1280]{0,1:T(8,128)} dynamic-update-slice(f32[6144,1280]{0,1:T(8,128)} %bitcast.14, f32[3072,1280]{0,1:T(8,128)} %bitcast_add_fusion, s32[]{:T(128)S(6)} %min.4, s32[]{:T(128)} %constant.57.clone.1) | dynamic-update-slice | bytes 31457284 | tf_op jit(solution)/shard_map/dynamic_update_slice | solution.py:56
  302.4 0.0 reduce-scatter.2.cloned.1.call-update
  302.4 0.0 all-gather.2.cloned.1.call-start
  302.5 185.3 %reduce-scatter.2.cloned.1.call-done = f32[768,1280]{0,1:T(8,128)} async-done(((f32[6144,1280]{0,1:T(8,128)}), f32[768,1280]{0,1:T(8,128)}) %reduce-scatter.2.cloned.1.call-update) | async-done | bytes 3932176 | tf_op jit(solution)/shard_map/reduce_scatter | solution.py:59
  487.7 3.6 convert_element_type.26
  491.3 0.0 all-gather.2.cloned.1.call-update
  491.3 0.2 all-reduce.2.cloned.1.call-start
  491.6 84.8 %all-gather.2.cloned.1.call-done = bf16[6144,1280]{0,1:T(8,128)(2,1)} async-done(((bf16[768,1280]{0,1:T(8,128)(2,1)}), bf16[6144,1280]{0,1:T(8,128)(2,1)}) %all-gather.2.cloned.1.call-update) | async-done | bytes 15728656 | tf_op jit(solution)/shard_map/all_gather | solution.py:62
  576.4 11.7 %dynamic-slice_select_fusion = bf16[3072,1280]{0,1:T(8,128)(2,1)} fusion(bf16[6144,1280]{0,1:T(8,128)(2,1)} %all-gather.2.cloned.1.call-done, s32[]{:T(128)S(6)} %select_n.60, pred[]{:T(512)S(6)} %eq.7), kind=kLoop, calls=%fused_computation.4 | loop fusion | flops 3932160 | bytes 15728645 | tf_op jit(solution)/shard_map/jit(_where)/select_n | solution.py:34
  588.1 0.0 all-reduce.2.cloned.1.call-update
  588.1 0.7 add_add_fusion.1
  588.9 0.8 add_add_fusion
  589.6 272.4 %all-reduce.2.cloned.1.call-done = bf16[3072,1280]{0,1:T(8,128)(2,1)} async-done(((bf16[3072,1280]{0,1:T(8,128)(2,1)}), bf16[3072,1280]{0,1:T(8,128)(2,1)}) %all-reduce.2.cloned.1.call-update) | async-done | bytes 7864336 | tf_op jit(solution)/shard_map/psum | solution.py:34
  862.0 63.1 %divide_convert_fusion = bf16[6144,3072]{1,0:T(8,128)(2,1)} fusion(bf16[6144,1280]{0,1:T(8,128)(2,1)} %all-gather.2.cloned.1.call-done, bf16[3072,1280]{0,1:T(8,128)(2,1)} %all-reduce.2.cloned.1.call-done, f32[3072]{0:T(1024)S(1)} %add_add_fusion.1, f32[6144]{0:T(1024)S(1)} %add_add_fusion), kind=kOutput, calls=%fused_computation.1 | convolution fusion | flops 48393879552 | bytes 61378560 | tf_op jit(solution)/shard_map/dot_general | solution.py:67
  (2 shorter events, 0.0 us)
Async XLA Ops:
  6.5 481.2 %reduce-scatter.2.cloned.1.call-start = ((), (), s32[]{:S(2)}) async-start(), calls=%async_computation.1 | async-start | bytes 35389440 | tf_op jit(solution)/shard_map/reduce_scatter | solution.py:59
  6.5 49.0 %collective-permute-start = (bf16[768,1280]{1,0:T(8,128)(2,1)}, bf16[768,1280]{1,0:T(8,128)(2,1)S(1)}, u32[]{:S(2)}, u32[]{:S(2)}) collective-permute-start(bf16[768,1280]{1,0:T(8,128)(2,1)} %param.5), channel_id=1, source_target_pairs={{0,1},{1,2},{2,3},{3,0},{4,5},{5,6},{6,7},{7,4},{8,9},{9,10},{10,1... | collective-permute-start | bytes 5898248 | tf_op jit(solution)/shard_map/ppermute | solution.py:23
  9.6 87.0 %collective-permute-start.2 = (bf16[768,1280]{1,0:T(8,128)(2,1)}, bf16[768,1280]{1,0:T(8,128)(2,1)}, u32[]{:S(2)}, u32[]{:S(2)}) collective-permute-start(bf16[768,1280]{1,0:T(8,128)(2,1)} %param.5), channel_id=1, source_target_pairs={{1,0},{2,1},{3,2},{0,3},{5,4},{6,5},{7,6},{4,7},{9,8},{10,9},{11,1... | collective-permute-start | bytes 5898248 | tf_op jit(solution)/shard_map/ppermute | solution.py:25
  55.5 83.5 %collective-permute-start.1 = (bf16[768,1280]{1,0:T(8,128)(2,1)S(1)}, bf16[768,1280]{1,0:T(8,128)(2,1)}, u32[]{:S(2)}, u32[]{:S(2)}) collective-permute-start(bf16[768,1280]{1,0:T(8,128)(2,1)S(1)} %collective-permute-done), channel_id=1, source_target_pairs={{0,1},{1,2},{2,3},{3,0},{4,5},{5,6},{6,7},{7,4},{8,9},{9,10},{10,1... | collective-permute-start | bytes 5898248 | tf_op jit(solution)/shard_map/ppermute | solution.py:23
  163.7 57.9 %copy-start = (bf16[3072,1280]{0,1:T(8,128)(2,1)S(1)}, bf16[3072,1280]{0,1:T(8,128)(2,1)}, u32[]{:S(2)}) copy-start(bf16[3072,1280]{0,1:T(8,128)(2,1)} %copy.6) | copy-start | bytes 23592964
  302.4 274.0 %all-gather.2.cloned.1.call-start = ((), (), s32[]{:S(2)}) async-start(), calls=%async_computation.2 | async-start | bytes 17694720 | tf_op jit(solution)/shard_map/all_gather | solution.py:62
  491.3 370.7 %all-reduce.2.cloned.1.call-start = ((), (), s32[]{:S(2)}) async-start(), calls=%async_computation.3 | async-start | bytes 15728640 | tf_op jit(solution)/shard_map/psum | solution.py:34
Sparse Core Ops, SparseCore 0:
  302.5 185.1 reduce-scatter.1
  491.4 84.9 all-gather.1
  588.2 273.7 all-reduce.1

commit v2 on v0

--- a/solution.py
+++ b/solution.py
@@ -9,7 +9,7 @@
 
 def broadcast(x, axis, root):
     mine = lax.axis_index(axis) == root
-    return lax.psum(jnp.where(mine, x, jnp.zeros_like(x)), axis)
+    return jnp.sum(lax.all_gather(jnp.where(mine, x, jnp.zeros_like(x)), axis), axis=0)
 
 
 def pair_gap(occ_map, vir_map):

time: 886 us -> 1150 us (1.30)
  waiting for transfers between devices: 694 us -> 947 us
  other arithmetic: 25.5 us -> 41.3 us
    all_gather x0 -> x1, waiting for transfers between devices: none -> 526 us  [broadcast(): lax.all_gather(jnp.where(mine, x, jnp.zeros_like(x)), axis)]
    psum x1 -> x0, waiting for transfers between devices: 272 us -> none  [broadcast(): return lax.psum(jnp.where(mine, x, jnp.zeros_like(x)), axis)]
    reduce_sum x0 -> x1, other arithmetic: none -> 15.8 us  [broadcast(): jnp.sum(lax.all_gather(jnp.where(mine, x, jnp.zeros_like(x)), axis), axis=0)]
where the time goes in v2:
time: 1150 us
  waiting for transfers between devices  947 us (82%)
  matrix products  115 us (10%)
  other arithmetic  41.3 us (4%)
  local copies, waits for them, and re-layouts  36.3 us (3%)
  between operations  13.2 us (1%)
    all_gather x1, waiting for transfers between devices, broadcast(): lax.all_gather(jnp.where(mine, x, jnp.zeros_like(x)), axis)  526 us
    reduce_scatter x1, waiting for transfers between devices, body(): lax.psum_scatter(partial_value, 'row', scatter_dimension=0, tiled=True)  190 us
    all_gather x1, waiting for transfers between devices, body(): piece = lax.all_gather(cholesky, 'col', axis=0, tiled=True)  145 us
    all_gather x1, waiting for transfers between devices, body(): y_block = lax.all_gather(y_share, 'row', axis=0, tiled=True)  85.2 us
    dot_general x1, matrix products, body(): total = jnp.dot(amplitudes, piece, preferred_element_type=jnp.float32)  58.6 us
    dot_general x1, matrix products, body(): lax.dot_general(y_block, y_cols, (((1,), (1,)), ((), ())), preferred_elem...  56.7 us
    dynamic_update_slice x1, local copies, waits for them, and re-layouts, body(): lax.dynamic_update_slice_in_dim(total, current + on_diag * piece.astype(j...  36.3 us
  transfers between devices with their start and end apart: 4, of which 4 were waited for; matrix products, arithmetic and copies ran while one was open for 0% of the time, Pallas kernels for 0%

profile of v2, /device:TPU:0, one launch (start us, length us, event | category | flops | bytes accessed | tf_op | source)
XLA Modules:
  0.0 1153.5 jit_solution(5886756732781477928)
XLA Ops:
  6.5 0.0 all-gather.5.cloned.1.call-start
  6.5 0.7 all-gather.5.cloned.1.call-update
  7.3 0.0 reduce-scatter.2.cloned.1.call-start
  7.3 145.4 %all-gather.5.cloned.1.call-done = bf16[3072,1280]{1,0:T(8,128)(2,1)} async-done(((bf16[768,1280]{1,0:T(8,128)(2,1)}), bf16[3072,1280]{1,0:T(8,128)(2,1)}) %all-gather.5.cloned.1.call-update) | async-done | bytes 7864336 | tf_op jit(solution)/shard_map/all_gather | solution.py:30
  152.7 0.0 copy-start
  152.7 58.6 %fusion = f32[6144,1280]{1,0:T(8,128)} fusion(bf16[6144,3072]{1,0:T(8,128)(2,1)} %param.4, bf16[3072,1280]{1,0:T(8,128)(2,1)} %all-gather.5.cloned.1.call-done), kind=kOutput, calls=%fused_computation.5 | convolution fusion | flops 48318382080 | bytes 77070336 | tf_op jit(solution)/shard_map/dot_general | solution.py:32
  211.3 0.0 copy-done
  211.3 11.6 %multiply_add_fusion = f32[3072,1280]{1,0:T(8,128)} fusion(bf16[3072,1280]{1,0:T(8,128)(2,1)S(1)} %copy-done, f32[6144,1280]{1,0:T(8,128)} %fusion, s32[]{:T(128)S(6)} %min.4, f32[]{:T(128)S(6)} %convert_element_type.26), kind=kLoop, calls=%fused_computation.1 | loop fusion | flops 11796480 | bytes 39321608 | tf_op jit(solution)/shard_map/add | solution.py:35
  222.9 36.3 %dynamic_update_slice.3 = f32[6144,1280]{1,0:T(8,128)} dynamic-update-slice(f32[6144,1280]{1,0:T(8,128)} %fusion, f32[3072,1280]{1,0:T(8,128)} %multiply_add_fusion, s32[]{:T(128)S(6)} %min.4, s32[]{:T(128)} %constant.42.clone.1) | dynamic-update-slice | bytes 31457284 | tf_op jit(solution)/shard_map/dynamic_update_slice | solution.py:34
  259.3 0.0 reduce-scatter.2.cloned.1.call-update
  259.3 0.0 all-gather.7.cloned.1.call-start
  259.4 190.0 %reduce-scatter.2.cloned.1.call-done = f32[768,1280]{1,0:T(8,128)} async-done(((f32[6144,1280]{1,0:T(8,128)}), f32[768,1280]{1,0:T(8,128)}) %reduce-scatter.2.cloned.1.call-update) | async-done | bytes 3932176 | tf_op jit(solution)/shard_map/reduce_scatter | solution.py:37
  449.3 3.6 convert_element_type.28
  452.9 0.0 all-gather.7.cloned.1.call-update
  452.9 0.2 all-gather.9.cloned.1.call-start
  453.2 85.2 %all-gather.7.cloned.1.call-done = bf16[6144,1280]{1,0:T(8,128)(2,1)} async-done(((bf16[768,1280]{1,0:T(8,128)(2,1)}), bf16[6144,1280]{1,0:T(8,128)(2,1)}) %all-gather.7.cloned.1.call-update) | async-done | bytes 15728656 | tf_op jit(solution)/shard_map/all_gather | solution.py:40
  538.4 8.8 dynamic-slice_select_fusion
  547.2 0.0 all-gather.9.cloned.1.call-update
  547.2 0.7 add_add_fusion.1
  548.0 0.8 add_add_fusion
  548.7 525.7 %all-gather.9.cloned.1.call-done = bf16[12288,1280]{1,0:T(8,128)(2,1)} async-done(((bf16[3072,1280]{1,0:T(8,128)(2,1)}), bf16[12288,1280]{1,0:T(8,128)(2,1)}) %all-gather.9.cloned.1.call-update) | async-done | bytes 31457296 | tf_op jit(solution)/shard_map/all_gather | solution.py:12
  1074.5 15.8 %reduce_sum.12 = bf16[3072,1280]{1,0:T(8,128)(2,1)} reduce(bf16[4,3072,1280]{2,1,0:T(8,128)(2,1)} %bitcast.5, bf16[]{:T(256)} %constant.49.clone.1), dimensions={0}, to_apply=%region_1.2 | reduce | flops 11796480 | bytes 39321600 | tf_op jit(solution)/shard_map/reduce_sum | solution.py:12
  1090.2 56.7 %divide_convert_fusion = bf16[6144,3072]{1,0:T(8,128)(2,1)} fusion(bf16[6144,1280]{1,0:T(8,128)(2,1)} %all-gather.7.cloned.1.call-done, bf16[3072,1280]{1,0:T(8,128)(2,1)} %reduce_sum.12, f32[3072]{0:T(1024)S(1)} %add_add_fusion.1, f32[6144]{0:T(1024)S(1)} %add_add_fusion), kind=kOutput, calls=%fused_computation | convolution fusion | flops 48393879552 | bytes 61378560 | tf_op jit(solution)/shard_map/dot_general | solution.py:45
Async XLA Ops:
  6.5 146.2 %all-gather.5.cloned.1.call-start = ((), (), s32[]{:S(2)}) async-start(), calls=%async_computation.1 | async-start | bytes 9830400 | tf_op jit(solution)/shard_map/all_gather | solution.py:30
  7.3 442.1 %reduce-scatter.2.cloned.1.call-start = ((), (), s32[]{:S(2)}) async-start(), calls=%async_computation.2 | async-start | bytes 35389440 | tf_op jit(solution)/shard_map/reduce_scatter | solution.py:37
  152.7 58.6 %copy-start = (bf16[3072,1280]{1,0:T(8,128)(2,1)S(1)}, bf16[3072,1280]{1,0:T(8,128)(2,1)}, u32[]{:S(2)}) copy-start(bf16[3072,1280]{1,0:T(8,128)(2,1)} %all-gather.5.cloned.1.call-done) | copy-start | bytes 23592964
  259.3 279.1 %all-gather.7.cloned.1.call-start = ((), (), s32[]{:S(2)}) async-start(), calls=%async_computation.3 | async-start | bytes 17694720 | tf_op jit(solution)/shard_map/all_gather | solution.py:40
  452.9 621.5 %all-gather.9.cloned.1.call-start = ((), (), s32[]{:S(2)}) async-start(), calls=%async_computation.4 | async-start | bytes 39321600 | tf_op jit(solution)/shard_map/all_gather | solution.py:12
Sparse Core Ops, SparseCore 0:
  8.9 143.7 all-gather.4
  259.4 189.8 reduce-scatter.1
  453.1 85.2 all-gather.6
  547.3 527.0 all-gather.8
